TPU v7x, 32 devices: a whole 2x2x4 slice. The times are simulated.
32 devices in a mesh: gx: 4 (over y, x), gy: 8 (over z, core).
Axes of the slice: x: 2, y: 2, z: 4, core: 2. Of those that a mesh axis runs over, the one named last changes fastest.
Arguments:
- basis_fields: float32 [128, 128, 1024], P(None, 'gx', 'gy'), may hold values from -6 to 6
- carried_fields: float32 [128, 128, 1024], P(None, 'gx', 'gy'), may hold values from -70 to 70, as said below
- velocity: float32 [2, 128, 1024], P(None, 'gx', 'gy'), may hold values from -1 to 1
- diffusion: float32 [128, 128], replicated, may hold values from -0.024 to 0.09, as said below
- advection: float32 [128, 128], replicated, may hold values from -0.18 to 0.18
Outputs:
- new_basis: float32 [256, 128, 1024], P(None, 'gx', 'gy')
- galerkin: float32 [256, 128], replicated
Inputs may be any that keep to these rules, and one draw needn't show every extreme that they name: `carried_fields`: entries of the field block are of order one with scales varying over cells and fields. `diffusion`: A positive diagonal with small couplings off it.
All inputs are finite; a program needn't handle non-finite values.
Results may differ from a plain program's by a relative error of at most 0.000086.
Values sent between devices are 32-bit elements; how exact they have to be, the bound alone decides.
No kernel may reach another device: no remote copies, remote signals or barrier semaphores. Data moves between devices by JAX's collectives and lax.ppermute only.
A program may use at most 64 MiB of HBM per device.

v0:
```python
import jax
import jax.numpy as jnp
from jax import lax
from jax.sharding import PartitionSpec as P


def extended(array, sides, width):
    for axis, dim in sides:
        count, length = (lax.axis_size(axis), array.shape[dim])
        up = [(i, (i + 1) % count) for i in range(count)]
        down = [(j, i) for i, j in up]
        last = lax.slice_in_dim(array, length - width, length, axis=dim)
        first = lax.slice_in_dim(array, 0, width, axis=dim)
        before = lax.ppermute(last, axis, up)
        after = lax.ppermute(first, axis, down)
        array = jnp.concatenate([before, array, after], axis=dim)
    return array


def field_rate(padded, velocity, diffusion, advection):
    center = padded[:, 1:-1, 1:-1]
    plus_x = padded[:, 2:, 1:-1]
    minus_x = padded[:, :-2, 1:-1]
    plus_y = padded[:, 1:-1, 2:]
    minus_y = padded[:, 1:-1, :-2]
    field_shape = center.shape
    laplace = plus_x + minus_x + plus_y + minus_y - 4.0 * center
    transport = velocity[0] * (plus_x - minus_x) * 0.5 + velocity[1] * (plus_y - minus_y) * 0.5
    spread_part = jnp.dot(
        diffusion.T, laplace.reshape(field_shape[0], -1), precision=lax.Precision.HIGHEST
    )
    carry_part = jnp.dot(
        advection.T, transport.reshape(field_shape[0], -1), precision=lax.Precision.HIGHEST
    )
    return (spread_part - carry_part).reshape(field_shape)


def one_substep(fields, velocity, diffusion, advection):
    padded = extended(fields, (("gx", 1), ("gy", 2)), 1)
    return fields + field_rate(padded, velocity, diffusion, advection)


def body(basis_fields, carried_fields, velocity, diffusion, advection):
    basis_rank, tile_rows, tile_cols = carried_fields.shape
    tile_cells = tile_rows * tile_cols
    aug_count = 2 * basis_rank
    cell_weight = 1.0 / (tile_cells * lax.axis_size("gx") * lax.axis_size("gy"))
    flat_basis = basis_fields.reshape(basis_rank, tile_cells)
    flat_carried = carried_fields.reshape(basis_rank, tile_cells)
    section_one = one_substep(carried_fields, velocity, diffusion, advection)
    section_two = one_substep(section_one, velocity, diffusion, advection)
    flat_new = section_two.reshape(basis_rank, tile_cells)
    stacked = jnp.concatenate([flat_basis, flat_new], 0)
    whole_sum = lax.psum(jnp.dot(stacked, stacked.T, precision=lax.Precision.HIGHEST), ("gx", "gy"))
    gram_matrix = whole_sum * cell_weight
    cholesky_low = jnp.linalg.cholesky(gram_matrix)
    identity = jnp.eye(aug_count, dtype=jnp.float32)
    inverse = jax.scipy.linalg.solve_triangular(cholesky_low, identity, lower=True)
    new_basis = jnp.dot(inverse, stacked, precision=lax.Precision.HIGHEST)
    galerkin = (
        lax.psum(jnp.dot(new_basis, flat_carried.T, precision=lax.Precision.HIGHEST), ("gx", "gy"))
        * cell_weight
    )
    return (new_basis.reshape(aug_count, tile_rows, tile_cols), galerkin)


def solution(mesh):
    in_specs = (P(None, "gx", "gy"), P(None, "gx", "gy"), P(None, "gx", "gy"), P(), P())
    out_specs = (P(None, "gx", "gy"), P())
    return jax.shard_map(body, mesh=mesh, in_specs=in_specs, out_specs=out_specs, check_vma=False)
```

profile of v0, /device:TPU:0, one launch (start us, length us, event | category | flops | bytes accessed | tf_op | source)
XLA Modules:
  0.0 395.5 jit_solution(6625425687016328248)
XLA Ops:
  7.2 2.0 copy.49
  9.3 3.0 collective-permute-start.1
  12.3 1.0 collective-permute-start
  13.3 3.5 copy.42
  17.0 1.9 pad_maximum_fusion.3
  18.9 2.7 collective-permute-start.2
  21.7 0.4 copy.44
  22.1 1.0 collective-permute-done.2
  23.2 3.5 collective-permute-done.3
  26.7 2.7 add_multiply_fusion.1
  29.4 1.9 fusion.22
  31.3 1.9 convolution_subtract_fusion.1
  33.5 1.6 collective-permute-start.4
  35.1 0.5 collective-permute-start.5
  35.6 2.2 collective-permute-done.4
  37.8 2.5 collective-permute-done.5
  40.4 0.8 collective-permute-start.7
  41.2 3.0 copy.36
  44.2 1.6 collective-permute-done.7
  45.8 2.8 multiply_subtract_fusion
  48.6 1.8 fusion.23
  50.5 4.2 %add_multiply_fusion = f32[128,32,128]{0,2,1:T(8,128)S(1)} fusion(f32[128,1,128]{0,2,1:T(8,128)S(1)} %collective-permute-done.4, f32[128,32,128]{0,2,1:T(8,128)S(1)} %add.63, f32[128,1,128]{0,2,1:T(8,128)S(1)} %collective-permute-done.5, f32[128,34,1]{0,2,1:T(1,128)S(1)} %copy.51, f32[128,34,1]{0,2,1:T(1,128)S(1)} %copy.53, ...), kind=kLoop, calls=%fused_computation.23 | loop fusion | flops 7340032 | bytes 4392960 | tf_op jit(solution)/shard_map/add | solution.py:28
  54.7 1.9 convolution_subtract_fusion
  56.6 0.3 add.68
  56.9 1.3 copy-done.5
  58.2 0.7 copy-done.7
  58.9 7.4 %fusion.1 = f32[256,256]{0,1:T(8,128)} fusion(f32[128,4096]{0,1:T(8,128)S(1)} %bitcast.71, f32[128,4096]{0,1:T(8,128)S(1)} %bitcast.75), kind=kOutput, calls=%fused_computation.6 | convolution fusion | flops 3222274048 | bytes 4456448 | tf_op jit(solution)/shard_map/dot_general | solution.py:54
  66.6 123.1 %all-reduce.4.cloned.1.call-done = f32[256,256]{0,1:T(8,128)} async-done(((f32[256,256]{0,1:T(8,128)}), f32[256,256]{0,1:T(8,128)}) %all-reduce.4.cloned.1.call-update) | async-done | bytes 262160 | tf_op jit(solution)/shard_map/psum | solution.py:54
  189.8 1.0 broadcast_multiply_fusion
  190.9 1.1 fusion.8
  192.0 11.7 %cholesky.50 = f32[128,128]{1,0:T(8,128)S(1)} custom-call(f32[128,128]{1,0:T(8,128)S(1)} %cholesky.118), custom_call_target="Cholesky" | custom-call | tf_op jit(solution)/shard_map/jit(cholesky)/cholesky | solution.py:56
  203.8 9.8 %custom-call.15 = f32[1,128,128]{1,2,0:T(8,128)S(1)} custom-call(f32[1,128,128]{2,1,0:T(8,128)S(1)} %get-tuple-element.33), custom_call_target="InvertDiagBlocksLowerTriangular" | custom-call | tf_op jit(solution)/shard_map/jit(cholesky)/cholesky | solution.py:56
  213.8 0.3 convolution_subtract_fusion.3
  214.1 11.7 %cholesky.105 = f32[128,128]{1,0:T(8,128)S(1)} custom-call(f32[128,128]{1,0:T(8,128)S(1)} %convolution_subtract_fusion.3), custom_call_target="Cholesky" | custom-call | tf_op jit(solution)/shard_map/jit(cholesky)/cholesky | solution.py:56
  225.8 0.7 compare_reduce_fusion
  227.9 4.1 %while.1 = (s32[]{:T(128)}, f32[256,256]{1,0:T(8,128)S(1)}, s32[2,2]{1,0:T(2,128)S(1)}, f32[2,128,128]{2,1,0:T(8,128)S(1)}, s32[]{:T(128)}) while((s32[]{:T(128)}, f32[256,256]{1,0:T(8,128)S(1)}, s32[2,2]{1,0:T(2,128)S(1)}, f32[2,128,128]{2,1,0:T(8,128)S(1)}, s32[]{:T(128)}) %tuple.33), condition=%wide.while_cond, body=%wide.while_body.sunk | while | flops 2 | bytes 131181 | solution.py:58
  228.1 0.6 fusion.38
  228.7 1.3 bitcast_dynamic-update-slice_fusion.2
  230.1 0.6 fusion.38
  230.7 1.3 bitcast_dynamic-update-slice_fusion.2
  232.0 19.7 %custom-call.16 = f32[2,128,128]{1,2,0:T(8,128)S(1)} custom-call(f32[2,128,128]{2,1,0:T(8,128)S(1)} %get-tuple-element.9), custom_call_target="InvertDiagBlocksLowerTriangular" | custom-call | tf_op jit(solution)/shard_map/jit(_solve_triangular)/triangular_solve | solution.py:58
  252.2 0.3 fusion.12
  252.6 5.8 %fusion = f32[256,4096]{1,0:T(8,128)S(1)} fusion(f32[128,4096]{0,1:T(8,128)S(1)} %bitcast.72, f32[128,4096]{0,1:T(8,128)} %bitcast.74, f32[128,256]{1,0:T(8,128)S(1)} %fusion.12, f32[128,256]{1,0:T(8,128)S(1)} %fusion.9), kind=kOutput, calls=%fused_computation.5 | convolution fusion | flops 3222339584 | bytes 8650752 | tf_op jit(solution)/shard_map/dot_general | solution.py:59
  258.4 1.9 copy-done.1
  260.3 4.9 %fusion.2 = f32[256,128]{1,0:T(8,128)} fusion(f32[256,4096]{1,0:T(8,128)S(1)} %fusion, f32[16,8,32,128]{3,2,1,0:T(8,128)S(1)} %bitcast.65), kind=kOutput, calls=%fused_computation.8 | convolution fusion | flops 1610612736 | bytes 6422528 | tf_op jit(solution)/shard_map/dot_general | solution.py:61
  265.3 5.0 %copy.57 = f32[32,8,32,128]{3,2,1,0:T(8,128)} copy(f32[32,8,32,128]{3,1,2,0:T(8,128)} %bitcast.64) | data formatting | bytes 8388608
  270.2 116.6 %all-reduce.6.cloned.1.call-done = f32[256,128]{1,0:T(8,128)} async-done(((f32[256,128]{1,0:T(8,128)}), f32[256,128]{1,0:T(8,128)}) %all-reduce.6.cloned.1.call-update) | async-done | bytes 131088 | tf_op jit(solution)/shard_map/psum | solution.py:61
  386.9 1.6 broadcast_multiply_fusion.1
  (53 shorter events, 2.1 us)
Async XLA Ops:
  7.2 22.2 %copy-start = (f32[128,128]{1,0:T(8,128)S(1)}, f32[128,128]{1,0:T(8,128)}, u32[]{:S(2)}) copy-start(f32[128,128]{1,0:T(8,128)} %param.8) | copy-start | bytes 196612
  7.2 182.6 %all-reduce.4.cloned.1.call-start = ((), (), s32[]{:S(2)}) async-start(), calls=%async_computation | async-start | bytes 524288 | tf_op jit(solution)/shard_map/psum | solution.py:54
  9.2 17.4 %copy-start.2 = (f32[128,32,128]{0,2,1:T(8,128)}, f32[128,32,128]{0,2,1:T(8,128)S(1)}, u32[]{:S(2)}) copy-start(f32[128,32,128]{0,2,1:T(8,128)S(1)} %copy.49) | copy-start | bytes 6291460
  9.3 7.5 %collective-permute-start.1 = (f32[128,1,128]{0,2,1:T(8,128)S(1)}, f32[128,1,128]{0,2,1:T(8,128)S(1)}, u32[]{:S(2)}, u32[]{:S(2)}) collective-permute-start(f32[128,1,128]{0,2,1:T(8,128)S(1)} %get-tuple-element.28), channel_id=1, source_target_pairs={{0,8},{8,16},{16,24},{24,0},{1,9},{9,17},{17,25},{25,1},{2,10},{10... | collective-permute-start | bytes 196616 | tf_op jit(solution)/shard_map/ppermute | solution.py:14
  12.3 4.7 %collective-permute-start = (f32[128,1,128]{0,2,1:T(8,128)S(1)}, f32[128,1,128]{0,2,1:T(8,128)S(1)}, u32[]{:S(2)}, u32[]{:S(2)}) collective-permute-start(f32[128,1,128]{0,2,1:T(8,128)S(1)} %get-tuple-element.29), channel_id=1, source_target_pairs={{8,0},{16,8},{24,16},{0,24},{9,1},{17,9},{25,17},{1,25},{10,2},{18... | collective-permute-start | bytes 196616 | tf_op jit(solution)/shard_map/ppermute | solution.py:15
  17.0 4.7 %copy-start.9 = (f32[2,32,128]{2,1,0:T(8,128)S(1)}, f32[2,32,128]{2,1,0:T(8,128)}, u32[]{:S(2)}) copy-start(f32[2,32,128]{2,1,0:T(8,128)} %param.7) | copy-start | bytes 98308
  18.9 4.2 %collective-permute-start.2 = (f32[128,34,1]{0,1,2:T(8,128)S(1)}, f32[128,34,1]{0,1,2:T(8,128)S(1)}, u32[]{:S(2)}, u32[]{:S(2)}) collective-permute-start(f32[128,34,1]{0,1,2:T(8,128)S(1)} %get-tuple-element.23), channel_id=1, source_target_pairs={{1,0},{2,1},{3,2},{4,3},{5,4},{6,5},{7,6},{0,7},{9,8},{10,9},{11,1... | collective-permute-start | bytes 52232 | tf_op jit(solution)/shard_map/ppermute | solution.py:15
  21.7 5.0 %collective-permute-start.3 = (f32[128,34,1]{0,1,2:T(8,128)S(1)}, f32[128,34,1]{0,1,2:T(8,128)S(1)}, u32[]{:S(2)}, u32[]{:S(2)}) collective-permute-start(f32[128,34,1]{0,1,2:T(8,128)S(1)} %get-tuple-element.22), channel_id=1, source_target_pairs={{0,1},{1,2},{2,3},{3,4},{4,5},{5,6},{6,7},{7,0},{8,9},{9,10},{10,1... | collective-permute-start | bytes 52232 | tf_op jit(solution)/shard_map/ppermute | solution.py:14
  29.4 1.9 copy-start.8
  31.3 1.9 copy-start.3
  33.5 4.3 %collective-permute-start.4 = (f32[128,1,128]{0,2,1:T(8,128)S(1)}, f32[128,1,128]{0,2,1:T(8,128)S(1)}, u32[]{:S(2)}, u32[]{:S(2)}) collective-permute-start(f32[128,1,128]{0,2,1:T(8,128)S(1)} %get-tuple-element.27), channel_id=1, source_target_pairs={{8,0},{16,8},{24,16},{0,24},{9,1},{17,9},{25,17},{1,25},{10,2},{18... | collective-permute-start | bytes 196616 | tf_op jit(solution)/shard_map/ppermute | solution.py:15
  35.1 5.2 %collective-permute-start.5 = (f32[128,1,128]{0,2,1:T(8,128)S(1)}, f32[128,1,128]{0,2,1:T(8,128)S(1)}, u32[]{:S(2)}, u32[]{:S(2)}) collective-permute-start(f32[128,1,128]{0,2,1:T(8,128)S(1)} %get-tuple-element.26), channel_id=1, source_target_pairs={{0,8},{8,16},{16,24},{24,0},{1,9},{9,17},{17,25},{25,1},{2,10},{10... | collective-permute-start | bytes 196616 | tf_op jit(solution)/shard_map/ppermute | solution.py:14
  40.3 3.8 collective-permute-start.6
  40.4 5.3 %collective-permute-start.7 = (f32[128,34,1]{0,1,2:T(8,128)S(1)}, f32[128,34,1]{0,1,2:T(8,128)S(1)}, u32[]{:S(2)}, u32[]{:S(2)}) collective-permute-start(f32[128,34,1]{0,1,2:T(8,128)S(1)} %copy.52), channel_id=1, source_target_pairs={{0,1},{1,2},{2,3},{3,4},{4,5},{5,6},{6,7},{7,0},{8,9},{9,10},{10,1... | collective-permute-start | bytes 52232 | tf_op jit(solution)/shard_map/ppermute | solution.py:14
  56.5 2.3 copy-start.7
  56.9 1.3 copy-start.5
  66.3 320.5 %all-reduce.6.cloned.1.call-start = ((), (), s32[]{:S(2)}) async-start(), calls=%async_computation.1 | async-start | bytes 262144 | tf_op jit(solution)/shard_map/psum | solution.py:61
  190.9 61.7 %copy-start.6 = (f32[128,32,128]{0,2,1:T(8,128)S(1)}, f32[128,32,128]{0,2,1:T(8,128)}, u32[]{:S(2)}) copy-start(f32[128,32,128]{0,2,1:T(8,128)} %copy-done.5) | copy-start | bytes 6291460
  252.6 7.8 %copy-start.4 = (f32[128,32,128]{2,1,0:T(8,128)S(1)}, f32[128,32,128]{2,1,0:T(8,128)}, u32[]{:S(2)}) copy-start(f32[128,32,128]{2,1,0:T(8,128)} %param.6) | copy-start | bytes 6291460
  258.3 2.0 copy-start.1
Sparse Core Ops, SparseCore 0:
  66.5 123.2 all-reduce.3
  265.4 121.4 all-reduce.5
where the time goes:
time: 402 us; the launch traced here: 395 us
  waiting for transfers between devices  251 us (62%)
  other arithmetic  69.7 us (17%)
  matrix products  26.9 us (7%)
  local copies, waits for them, and re-layouts  22 us (5%)
  between operations  15.9 us (4%)
  starting transfers between devices  9.9 us (2%)
    psum x1, waiting for transfers between devices, body(): lax.psum(jnp.dot(stacked, stacked.T, precision=lax.Precision.HIGHEST), ('...  123 us
    psum x1, waiting for transfers between devices, body(): lax.psum(jnp.dot(new_basis, flat_carried.T, precision=lax.Precision.HIGHE...  117 us
    another operation x6, other arithmetic, body(): cholesky_low = jnp.linalg.cholesky(gram_matrix)  34 us
    another operation x3, other arithmetic, body(): jax.scipy.linalg.solve_triangular(cholesky_low, identity, lower=True)  19.7 us
    unnamed x24, local copies, waits for them, and re-layouts  17.4 us
  transfers between devices with their start and end apart: 10, of which 8 were waited for; matrix products, arithmetic and copies ran while one was open for 3% of the time, Pallas kernels for 0%

commit v1 on v0

--- a/solution.py
+++ b/solution.py
@@ -57,8 +57,16 @@
     identity = jnp.eye(aug_count, dtype=jnp.float32)
     inverse = jax.scipy.linalg.solve_triangular(cholesky_low, identity, lower=True)
     new_basis = jnp.dot(inverse, stacked, precision=lax.Precision.HIGHEST)
+
+    def proceed_the_patch(v0, row_axis, mesh_name):
+        for dd in (row_axis, mesh_name):
+            v0 = jax.lax.psum(v0, dd)
+        return v0
+
     galerkin = (
-        lax.psum(jnp.dot(new_basis, flat_carried.T, precision=lax.Precision.HIGHEST), ("gx", "gy"))
+        proceed_the_patch(
+            jnp.dot(new_basis, flat_carried.T, precision=lax.Precision.HIGHEST), "gy", "gx"
+        )
         * cell_weight
     )
     return (new_basis.reshape(aug_count, tile_rows, tile_cols), galerkin)

time: 402 us -> 377 us (0.938)
  waiting for transfers between devices: 251 us -> 227 us
    psum x1 -> x2, waiting for transfers between devices: 117 us -> 92.6 us  [proceed_the_patch(): v0 = jax.lax.psum(v0, dd)]
  transfers between devices with their start and end apart: 10 -> 11, of which waited for: 8 -> 9; matrix products, arithmetic and copies ran while one was open for 3% -> 3% of each run, Pallas kernels for 0% -> 0%
where the time goes in v1:
time: 377 us; the launch traced here: 371 us
  waiting for transfers between devices  227 us (60%)
  other arithmetic  69.7 us (18%)
  matrix products  26.9 us (7%)
  local copies, waits for them, and re-layouts  22 us (6%)
  between operations  15.6 us (4%)
  starting transfers between devices  9.94 us (3%)
    psum x1, waiting for transfers between devices, body(): lax.psum(jnp.dot(stacked, stacked.T, precision=lax.Precision.HIGHEST), ('...  123 us
    psum x2, waiting for transfers between devices, proceed_the_patch(): v0 = jax.lax.psum(v0, dd)  92.6 us
    another operation x6, other arithmetic, body(): cholesky_low = jnp.linalg.cholesky(gram_matrix)  34 us
    another operation x3, other arithmetic, body(): jax.scipy.linalg.solve_triangular(cholesky_low, identity, lower=True)  19.7 us
    unnamed x24, local copies, waits for them, and re-layouts  17.4 us
  transfers between devices with their start and end apart: 11, of which 9 were waited for; matrix products, arithmetic and copies ran while one was open for 3% of the time, Pallas kernels for 0%

profile of v1, /device:TPU:0, one launch (start us, length us, event | category | flops | bytes accessed | tf_op | source)
XLA Modules:
  0.0 371.2 jit_solution(12774367034640296641)
XLA Ops:
  7.2 2.0 copy.49
  9.3 3.0 collective-permute-start.1
  12.3 1.0 collective-permute-start
  13.3 3.5 copy.42
  17.0 1.9 pad_maximum_fusion.3
  18.9 2.7 collective-permute-start.2
  21.7 0.4 copy.44
  22.1 1.0 collective-permute-done.2
  23.2 3.5 collective-permute-done.3
  26.7 2.7 add_multiply_fusion.1
  29.4 1.9 fusion.22
  31.3 1.9 convolution_subtract_fusion.1
  33.5 1.6 collective-permute-start.4
  35.1 0.5 collective-permute-start.5
  35.6 2.2 collective-permute-done.4
  37.8 2.5 collective-permute-done.5
  40.4 0.8 collective-permute-start.7
  41.2 3.0 copy.36
  44.2 1.6 collective-permute-done.7
  45.8 2.8 multiply_subtract_fusion
  48.6 1.8 fusion.23
  50.5 4.2 %add_multiply_fusion = f32[128,32,128]{0,2,1:T(8,128)S(1)} fusion(f32[128,1,128]{0,2,1:T(8,128)S(1)} %collective-permute-done.4, f32[128,32,128]{0,2,1:T(8,128)S(1)} %add.65, f32[128,1,128]{0,2,1:T(8,128)S(1)} %collective-permute-done.5, f32[128,34,1]{0,2,1:T(1,128)S(1)} %copy.51, f32[128,34,1]{0,2,1:T(1,128)S(1)} %copy.53, ...), kind=kLoop, calls=%fused_computation.23 | loop fusion | flops 7340032 | bytes 4392960 | tf_op jit(solution)/shard_map/add | solution.py:28
  54.7 1.9 convolution_subtract_fusion
  56.6 0.3 add.70
  56.9 1.3 copy-done.5
  58.2 0.7 copy-done.7
  58.9 7.4 %fusion.1 = f32[256,256]{0,1:T(8,128)} fusion(f32[128,4096]{0,1:T(8,128)S(1)} %bitcast.71, f32[128,4096]{0,1:T(8,128)S(1)} %bitcast.75), kind=kOutput, calls=%fused_computation.6 | convolution fusion | flops 3222274048 | bytes 4456448 | tf_op jit(solution)/shard_map/dot_general | solution.py:54
  66.6 123.1 %all-reduce.5.cloned.1.call-done = f32[256,256]{0,1:T(8,128)} async-done(((f32[256,256]{0,1:T(8,128)}), f32[256,256]{0,1:T(8,128)}) %all-reduce.5.cloned.1.call-update) | async-done | bytes 262160 | tf_op jit(solution)/shard_map/psum | solution.py:54
  189.8 1.0 broadcast_multiply_fusion
  190.9 1.1 fusion.8
  192.0 11.7 %cholesky.50 = f32[128,128]{1,0:T(8,128)S(1)} custom-call(f32[128,128]{1,0:T(8,128)S(1)} %cholesky.118), custom_call_target="Cholesky" | custom-call | tf_op jit(solution)/shard_map/jit(cholesky)/cholesky | solution.py:56
  203.8 9.8 %custom-call.15 = f32[1,128,128]{1,2,0:T(8,128)S(1)} custom-call(f32[1,128,128]{2,1,0:T(8,128)S(1)} %get-tuple-element.33), custom_call_target="InvertDiagBlocksLowerTriangular" | custom-call | tf_op jit(solution)/shard_map/jit(cholesky)/cholesky | solution.py:56
  214.1 11.7 %cholesky.105 = f32[128,128]{1,0:T(8,128)S(1)} custom-call(f32[128,128]{1,0:T(8,128)S(1)} %convolution_subtract_fusion.3), custom_call_target="Cholesky" | custom-call | tf_op jit(solution)/shard_map/jit(cholesky)/cholesky | solution.py:56
  225.8 0.7 compare_reduce_fusion
  227.9 4.1 %while.1 = (s32[]{:T(128)}, f32[256,256]{1,0:T(8,128)S(1)}, s32[2,2]{1,0:T(2,128)S(1)}, f32[2,128,128]{2,1,0:T(8,128)S(1)}, s32[]{:T(128)}) while((s32[]{:T(128)}, f32[256,256]{1,0:T(8,128)S(1)}, s32[2,2]{1,0:T(2,128)S(1)}, f32[2,128,128]{2,1,0:T(8,128)S(1)}, s32[]{:T(128)}) %tuple.33), condition=%wide.while_cond, body=%wide.while_body.sunk | while | flops 2 | bytes 131181 | solution.py:58
  228.1 0.6 fusion.38
  228.7 1.3 bitcast_dynamic-update-slice_fusion.2
  230.1 0.6 fusion.38
  230.7 1.3 bitcast_dynamic-update-slice_fusion.2
  232.0 19.7 %custom-call.16 = f32[2,128,128]{1,2,0:T(8,128)S(1)} custom-call(f32[2,128,128]{2,1,0:T(8,128)S(1)} %get-tuple-element.9), custom_call_target="InvertDiagBlocksLowerTriangular" | custom-call | tf_op jit(solution)/shard_map/jit(_solve_triangular)/triangular_solve | solution.py:58
  252.2 0.3 fusion.12
  252.6 5.8 %fusion = f32[256,4096]{1,0:T(8,128)S(1)} fusion(f32[128,4096]{0,1:T(8,128)S(1)} %bitcast.72, f32[128,4096]{0,1:T(8,128)} %bitcast.74, f32[128,256]{1,0:T(8,128)S(1)} %fusion.12, f32[128,256]{1,0:T(8,128)S(1)} %fusion.9), kind=kOutput, calls=%fused_computation.5 | convolution fusion | flops 3222339584 | bytes 8650752 | tf_op jit(solution)/shard_map/dot_general | solution.py:59
  258.4 1.9 copy-done.1
  260.3 4.9 %fusion.2 = f32[256,128]{1,0:T(8,128)} fusion(f32[256,4096]{1,0:T(8,128)S(1)} %fusion, f32[16,8,32,128]{3,2,1,0:T(8,128)S(1)} %bitcast.65), kind=kOutput, calls=%fused_computation.8 | convolution fusion | flops 1610612736 | bytes 6422528 | tf_op jit(solution)/shard_map/dot_general | solution.py:68
  265.3 53.4 %all-reduce.7.cloned.1.call-done = f32[256,128]{1,0:T(8,128)} async-done(((f32[256,128]{1,0:T(8,128)}), f32[256,128]{1,0:T(8,128)}) %all-reduce.7.cloned.1.call-update) | async-done | bytes 131088 | tf_op jit(solution)/shard_map/psum | solution.py:63
  318.7 5.0 %copy.57 = f32[32,8,32,128]{3,2,1,0:T(8,128)} copy(f32[32,8,32,128]{3,1,2,0:T(8,128)} %bitcast.64) | data formatting | bytes 8388608
  323.7 39.2 %all-reduce.9.cloned.1.call-done = f32[256,128]{1,0:T(8,128)} async-done(((f32[256,128]{1,0:T(8,128)}), f32[256,128]{1,0:T(8,128)}) %all-reduce.9.cloned.1.call-update) | async-done | bytes 131088 | tf_op jit(solution)/shard_map/psum | solution.py:63
  362.8 1.6 broadcast_multiply_fusion.1
  (56 shorter events, 2.5 us)
Async XLA Ops:
  7.2 22.2 %copy-start = (f32[128,128]{1,0:T(8,128)S(1)}, f32[128,128]{1,0:T(8,128)}, u32[]{:S(2)}) copy-start(f32[128,128]{1,0:T(8,128)} %param.8) | copy-start | bytes 196612
  7.2 182.6 %all-reduce.5.cloned.1.call-start = ((), (), s32[]{:S(2)}) async-start(), calls=%async_computation | async-start | bytes 524288 | tf_op jit(solution)/shard_map/psum | solution.py:54
  9.2 17.4 %copy-start.2 = (f32[128,32,128]{0,2,1:T(8,128)}, f32[128,32,128]{0,2,1:T(8,128)S(1)}, u32[]{:S(2)}) copy-start(f32[128,32,128]{0,2,1:T(8,128)S(1)} %copy.49) | copy-start | bytes 6291460
  9.3 7.5 %collective-permute-start.1 = (f32[128,1,128]{0,2,1:T(8,128)S(1)}, f32[128,1,128]{0,2,1:T(8,128)S(1)}, u32[]{:S(2)}, u32[]{:S(2)}) collective-permute-start(f32[128,1,128]{0,2,1:T(8,128)S(1)} %get-tuple-element.28), channel_id=1, source_target_pairs={{0,8},{8,16},{16,24},{24,0},{1,9},{9,17},{17,25},{25,1},{2,10},{10... | collective-permute-start | bytes 196616 | tf_op jit(solution)/shard_map/ppermute | solution.py:14
  12.3 4.7 %collective-permute-start = (f32[128,1,128]{0,2,1:T(8,128)S(1)}, f32[128,1,128]{0,2,1:T(8,128)S(1)}, u32[]{:S(2)}, u32[]{:S(2)}) collective-permute-start(f32[128,1,128]{0,2,1:T(8,128)S(1)} %get-tuple-element.29), channel_id=1, source_target_pairs={{8,0},{16,8},{24,16},{0,24},{9,1},{17,9},{25,17},{1,25},{10,2},{18... | collective-permute-start | bytes 196616 | tf_op jit(solution)/shard_map/ppermute | solution.py:15
  17.0 4.7 %copy-start.9 = (f32[2,32,128]{2,1,0:T(8,128)S(1)}, f32[2,32,128]{2,1,0:T(8,128)}, u32[]{:S(2)}) copy-start(f32[2,32,128]{2,1,0:T(8,128)} %param.7) | copy-start | bytes 98308
  18.9 4.2 %collective-permute-start.2 = (f32[128,34,1]{0,1,2:T(8,128)S(1)}, f32[128,34,1]{0,1,2:T(8,128)S(1)}, u32[]{:S(2)}, u32[]{:S(2)}) collective-permute-start(f32[128,34,1]{0,1,2:T(8,128)S(1)} %get-tuple-element.23), channel_id=1, source_target_pairs={{1,0},{2,1},{3,2},{4,3},{5,4},{6,5},{7,6},{0,7},{9,8},{10,9},{11,1... | collective-permute-start | bytes 52232 | tf_op jit(solution)/shard_map/ppermute | solution.py:15
  21.7 5.0 %collective-permute-start.3 = (f32[128,34,1]{0,1,2:T(8,128)S(1)}, f32[128,34,1]{0,1,2:T(8,128)S(1)}, u32[]{:S(2)}, u32[]{:S(2)}) collective-permute-start(f32[128,34,1]{0,1,2:T(8,128)S(1)} %get-tuple-element.22), channel_id=1, source_target_pairs={{0,1},{1,2},{2,3},{3,4},{4,5},{5,6},{6,7},{7,0},{8,9},{9,10},{10,1... | collective-permute-start | bytes 52232 | tf_op jit(solution)/shard_map/ppermute | solution.py:14
  29.4 1.9 copy-start.8
  31.3 1.9 copy-start.3
  33.5 4.3 %collective-permute-start.4 = (f32[128,1,128]{0,2,1:T(8,128)S(1)}, f32[128,1,128]{0,2,1:T(8,128)S(1)}, u32[]{:S(2)}, u32[]{:S(2)}) collective-permute-start(f32[128,1,128]{0,2,1:T(8,128)S(1)} %get-tuple-element.27), channel_id=1, source_target_pairs={{8,0},{16,8},{24,16},{0,24},{9,1},{17,9},{25,17},{1,25},{10,2},{18... | collective-permute-start | bytes 196616 | tf_op jit(solution)/shard_map/ppermute | solution.py:15
  35.1 5.2 %collective-permute-start.5 = (f32[128,1,128]{0,2,1:T(8,128)S(1)}, f32[128,1,128]{0,2,1:T(8,128)S(1)}, u32[]{:S(2)}, u32[]{:S(2)}) collective-permute-start(f32[128,1,128]{0,2,1:T(8,128)S(1)} %get-tuple-element.26), channel_id=1, source_target_pairs={{0,8},{8,16},{16,24},{24,0},{1,9},{9,17},{17,25},{25,1},{2,10},{10... | collective-permute-start | bytes 196616 | tf_op jit(solution)/shard_map/ppermute | solution.py:14
  40.3 3.8 %collective-permute-start.6 = (f32[128,34,1]{0,1,2:T(8,128)S(1)}, f32[128,34,1]{0,1,2:T(8,128)S(1)}, u32[]{:S(2)}, u32[]{:S(2)}) collective-permute-start(f32[128,34,1]{0,1,2:T(8,128)S(1)} %copy.50), channel_id=1, source_target_pairs={{1,0},{2,1},{3,2},{4,3},{5,4},{6,5},{7,6},{0,7},{9,8},{10,9},{11,1... | collective-permute-start | bytes 52232 | tf_op jit(solution)/shard_map/ppermute | solution.py:15
  40.4 5.3 %collective-permute-start.7 = (f32[128,34,1]{0,1,2:T(8,128)S(1)}, f32[128,34,1]{0,1,2:T(8,128)S(1)}, u32[]{:S(2)}, u32[]{:S(2)}) collective-permute-start(f32[128,34,1]{0,1,2:T(8,128)S(1)} %copy.52), channel_id=1, source_target_pairs={{0,1},{1,2},{2,3},{3,4},{4,5},{5,6},{6,7},{7,0},{8,9},{9,10},{10,1... | collective-permute-start | bytes 52232 | tf_op jit(solution)/shard_map/ppermute | solution.py:14
  56.5 2.3 copy-start.7
  56.9 1.3 copy-start.5
  66.3 252.3 %all-reduce.7.cloned.1.call-start = ((), (), s32[]{:S(2)}) async-start(), calls=%async_computation.1 | async-start | bytes 262144 | tf_op jit(solution)/shard_map/psum | solution.py:63
  190.9 61.7 %copy-start.6 = (f32[128,32,128]{0,2,1:T(8,128)S(1)}, f32[128,32,128]{0,2,1:T(8,128)}, u32[]{:S(2)}) copy-start(f32[128,32,128]{0,2,1:T(8,128)} %copy-done.5) | copy-start | bytes 6291460
  252.6 7.8 %copy-start.4 = (f32[128,32,128]{2,1,0:T(8,128)S(1)}, f32[128,32,128]{2,1,0:T(8,128)}, u32[]{:S(2)}) copy-start(f32[128,32,128]{2,1,0:T(8,128)} %param.6) | copy-start | bytes 6291460
  258.3 2.0 copy-start.1
  265.3 97.6 %all-reduce.9.cloned.1.call-start = ((), (), s32[]{:S(2)}) async-start(), calls=%async_computation.2 | async-start | bytes 262144 | tf_op jit(solution)/shard_map/psum | solution.py:63
Sparse Core Ops, SparseCore 0:
  66.5 123.2 all-reduce.4
  265.4 53.2 all-reduce.6
  321.8 40.9 all-reduce.8
